TPU v7x, 32 devices: a whole 2x2x4 slice. The times are simulated.
32 devices in a mesh: batch: 2 (over x), rows: 16 (over z, y, core).
Axes of the slice: x: 2, y: 2, z: 4, core: 2. Of those that a mesh axis runs over, the one named last changes fastest.
Arguments:
- layer_input: bfloat16 [2, 64, 64, 2048], P('batch', 'rows'), may hold values from -6 to 6
- pre_activation: bfloat16 [2, 64, 64, 2048], P('batch', 'rows'), may hold values from -6 to 6
- cotangent: bfloat16 [2, 64, 64, 2048], P('batch', 'rows'), may hold values from -6 to 6
- weight: bfloat16 [64, 64], replicated, may hold values from -0.75 to 0.75
- spectral: bfloat16 [2304, 64, 128], P('rows'), may hold values from -6 to 6
- slab_ids: int32 [2, 32], P('batch'), may hold values from 0 to 2047, as said below
- extents: int32 [2, 32], P('batch'), may hold values from 1 to 2048, as said below
Outputs:
- grad_input: bfloat16 [2, 64, 64, 2048], P('batch', 'rows')
- grad_spectral: float32 [2304, 64, 128], P('rows')
- grad_weight: float32 [64, 64], replicated
Inputs may be any that keep to these rules, and one draw needn't show every extreme that they name: `slab_ids`: within a sample the 32 slab numbers are distinct and include 0 and 2047; slots 2 k to 2 k + 1 are stored on index k of rows. `extents`: A slot's extent counts its slab's live columns from column 0.
All inputs are finite; a program needn't handle non-finite values.
Results may differ from a plain program's by a relative error of at most 0.0085.
Values may be sent and summed in bfloat16 or wider, within the bound.
No kernel may reach another device: no remote copies, remote signals or barrier semaphores. Data moves between devices by JAX's collectives and lax.ppermute only.
A program may use at most 128 MiB of HBM per device.

v0:
```python
import math
import jax
import jax.numpy as jnp
from jax import lax
from jax.sharding import PartitionSpec as P

PA = 48
SLAB = 2
NR = 4096
MODES = 96


def column_table(column_count, freq_count):
    column_index = jnp.arange(column_count, dtype=jnp.int32)
    freq_index = jnp.arange(freq_count, dtype=jnp.int32)
    phase = column_index[:, None] * freq_index[None, :] % column_count
    angle = phase.astype(jnp.float32) * (2.0 * math.pi / column_count)
    return jnp.concatenate([jnp.cos(angle), -jnp.sin(angle)], axis=1).astype(jnp.bfloat16)


def row_table(positions, row_total, freq_count):
    freq_index = jnp.arange(freq_count, dtype=jnp.int32) - freq_count // 2
    phase = jnp.mod(freq_index[:, None] * positions[None, :], row_total)
    angle = phase.astype(jnp.float32) * (2.0 * math.pi / row_total)
    return jnp.concatenate([jnp.cos(angle), jnp.sin(angle)], axis=0).astype(jnp.bfloat16)


def stored_positions(slab_list, slab_rows):
    offsets = jnp.tile(jnp.arange(slab_rows, dtype=jnp.int32), slab_list.shape[0])
    return jnp.repeat(slab_list, slab_rows) * slab_rows + offsets


def gelu_slope(values):
    return (
        0.5 * (1.0 + lax.erf(values * 0.7071067811865476))
        + values * jnp.exp(-0.5 * values * values) * 0.3989422804014327
    )


def row_combine(row_sums, scale):
    upper = row_sums[0]
    lower = row_sums[1]
    real_part = upper[:, :, 0] + lower[:, :, 1]
    imag_part = upper[:, :, 1] - lower[:, :, 0]
    return (jnp.stack([real_part, imag_part], axis=2) * scale).astype(jnp.bfloat16)


def to_blocks(spectra, half_modes):
    chans = spectra.shape[1]
    shaped = spectra.reshape(half_modes, 2, chans, 2, half_modes, 2)
    return shaped.transpose(2, 3, 1, 5, 0, 4).reshape(chans, 2, 2, 2, half_modes * half_modes)


def from_blocks(blocked, half_modes):
    chans = blocked.shape[0]
    shaped = blocked.reshape(chans, 2, 2, 2, half_modes, half_modes)
    return shaped.transpose(4, 2, 0, 1, 5, 3).reshape(2 * half_modes, chans, 2, 2 * half_modes)


def factor_pair(owned, chans):
    input_modes = owned[:chans]
    grad_out = owned[chans:]
    factor_left = input_modes.transpose(4, 0, 1, 2, 3).reshape(owned.shape[4], chans, 8)
    real_out = grad_out[:, 0]
    imag_out = grad_out[:, 1]
    first_half = jnp.stack([real_out, imag_out], axis=1)
    second_half = jnp.stack([imag_out, -real_out], axis=1)
    stacked = jnp.concatenate([first_half, second_half], axis=0)
    factor_right = stacked.transpose(4, 0, 1, 2, 3).reshape(owned.shape[4], 2 * chans, 8)
    return (factor_left, factor_right)


def modes_to_channels(grad_modes):
    blocks = grad_modes.shape[0]
    chans = grad_modes.shape[1]
    return grad_modes.reshape(blocks, chans, 2, 2, 2).transpose(1, 2, 3, 4, 0)


def row_adjoint(rowtab, grad_grid, scale):
    real_part = grad_grid[:, :, 0]
    imag_part = grad_grid[:, :, 1]
    upper = jnp.stack([real_part, imag_part], axis=2)
    lower = jnp.stack([-imag_part, real_part], axis=2)
    joined = jnp.concatenate([upper, lower], axis=0)
    summed = jnp.dot(
        rowtab.T, joined.reshape(joined.shape[0], -1), preferred_element_type=jnp.float32
    )
    return (summed * scale).astype(jnp.bfloat16)


def shards(layer_input, pre_activation, cotangent, weight, spectral, slab_ids, extents):
    batch_devices = lax.axis_size("batch")
    local_rows = layer_input.shape[1]
    channels = layer_input.shape[2]
    column_count = layer_input.shape[3]
    slab_list = slab_ids[0]
    active = slab_list.shape[0]
    slots = local_rows // SLAB
    scale = 1.0 / math.sqrt(NR * column_count)
    position = lax.axis_index("rows")
    own_extents = lax.dynamic_slice_in_dim(extents[0], position * slots, slots)
    column_index = jnp.arange(column_count, dtype=jnp.int32)
    alive = column_index[None, :] < jnp.repeat(own_extents, SLAB)[:, None]
    mask_half = alive.astype(jnp.bfloat16)
    mask_full = alive.astype(jnp.float32)
    masked_in = layer_input[0] * mask_half[:, None, :]
    grad_pre = (
        cotangent[0].astype(jnp.float32)
        * mask_full[:, None, :]
        * gelu_slope(pre_activation[0].astype(jnp.float32))
    ).astype(jnp.bfloat16)
    coltab = column_table(column_count, MODES)
    stacked = jnp.concatenate([masked_in, grad_pre], axis=1)
    colspec = jnp.dot(stacked.reshape(-1, column_count), coltab, preferred_element_type=jnp.float32)
    colspec = colspec.reshape(local_rows, 2 * channels, 2 * MODES).astype(jnp.bfloat16)
    gathered_rows = lax.all_to_all(colspec, "rows", split_axis=1, concat_axis=0, tiled=True)
    all_rows = gathered_rows.shape[0]
    owned_channels = gathered_rows.shape[1]
    rowtab = row_table(stored_positions(slab_list, SLAB), NR, MODES)
    row_sums = jnp.dot(
        rowtab, gathered_rows.reshape(all_rows, -1), preferred_element_type=jnp.float32
    )
    spectra = row_combine(row_sums.reshape(2, MODES, owned_channels, 2, MODES), scale)
    owned = lax.all_to_all(to_blocks(spectra, PA), "rows", split_axis=4, concat_axis=0, tiled=True)
    factor_left, factor_right = factor_pair(owned, channels)
    grad_modes = jnp.einsum(
        "bix,bxk->bik", spectral, factor_right, preferred_element_type=jnp.float32
    ).astype(jnp.bfloat16)
    own_grad = jnp.einsum(
        "bik,bxk->bix", factor_left, factor_right, preferred_element_type=jnp.float32
    )
    grad_spectral = lax.psum(own_grad, "batch")
    returned = lax.all_to_all(
        modes_to_channels(grad_modes), "rows", split_axis=0, concat_axis=4, tiled=True
    )
    rowback = row_adjoint(rowtab, from_blocks(returned, PA), scale)
    rowback = rowback.reshape(all_rows, -1, 2 * MODES)
    local_back = lax.all_to_all(rowback, "rows", split_axis=0, concat_axis=1, tiled=True)
    spatial = jnp.dot(
        local_back.reshape(-1, 2 * MODES), coltab.T, preferred_element_type=jnp.float32
    )
    spatial = spatial.reshape(local_rows, channels, column_count)
    row_weight = jnp.broadcast_to(weight, (local_rows, channels, channels))
    direct = jnp.einsum("rio,roc->ric", row_weight, grad_pre, preferred_element_type=jnp.float32)
    grad_input = ((spatial + direct) * mask_full[:, None, :]).astype(jnp.bfloat16)[None]
    row_partial = jnp.einsum(
        "ric,roc->rio", masked_in, grad_pre, preferred_element_type=jnp.float32
    )
    local_weight = jnp.sum(row_partial, axis=0)
    grad_weight = lax.psum(local_weight, ("batch", "rows"))
    grad_weight = grad_weight * (1.0 / math.sqrt(batch_devices * active * SLAB * column_count))
    return (grad_input, grad_spectral, grad_weight)


def solution(mesh):
    return jax.shard_map(
        shards,
        mesh=mesh,
        in_specs=(
            P("batch", "rows", None, None),
            P("batch", "rows", None, None),
            P("batch", "rows", None, None),
            P(),
            P("rows", None, None),
            P("batch", None),
            P("batch", None),
        ),
        out_specs=(P("batch", "rows", None, None), P("rows", None, None), P()),
        check_vma=False,
    )
```

profile of v0, /device:TPU:0, one launch (start us, length us, event | category | flops | bytes accessed | tf_op | source)
XLA Modules:
  0.0 304.3 jit_solution(13098841507869636662)
XLA Ops:
  18.4 7.5 %all-to-all-start = ((bf16[4,128,192]{2,0,1:T(4,128)(2,1)}), bf16[4,128,192]{2,0,1:T(4,128)(2,1)}, u32[]{:S(2)}, u32[]{:S(2)}) async-start(bf16[4,128,192]{2,0,1:T(4,128)(2,1)} %copy.52), calls=%async_computation | async-start | bytes 524288 | tf_op jit(solution)/shard_map/all_to_all | solution.py:116
  26.6 9.3 %all-to-all-done = bf16[4,128,192]{2,0,1:T(4,128)(2,1)} async-done(((bf16[4,128,192]{2,0,1:T(4,128)(2,1)}), bf16[4,128,192]{2,0,1:T(4,128)(2,1)}, u32[]{:S(2)}, u32[]{:S(2)}) %all-to-all-start) | async-done | bytes 196640 | tf_op jit(solution)/shard_map/all_to_all | solution.py:116
  47.9 4.2 %copy.79 = f32[96,8,1,96]{1,3,0,2:T(8,128)} copy(f32[96,8,1,96]{3,2,1,0:T(1,128)} %get-tuple-element.10) | data formatting | bytes 589824
  58.0 4.2 %copy.80 = f32[96,8,1,96]{1,3,0,2:T(8,128)} copy(f32[96,8,1,96]{3,2,1,0:T(1,128)} %get-tuple-element.8) | data formatting | bytes 589824
  62.2 6.9 %sub.9 = f32[96,8,1,96]{1,3,0,2:T(8,128)} subtract(f32[96,8,1,96]{1,3,0,2:T(8,128)} %copy.79, f32[96,8,1,96]{1,3,0,2:T(8,128)} %copy.80) | non-fusion elementwise | flops 73728 | bytes 884736 | tf_op jit(solution)/shard_map/sub | solution.py:44
  69.1 6.2 %copy.60 = f32[48,2,8,1,48,2]{4,2,5,3,1,0:T(8,128)} copy(f32[48,2,8,1,48,2]{2,5,4,1,0,3:T(2,128)} %bitcast.84) | data formatting | bytes 589824 | tf_op jit(solution)/shard_map/stack | solution.py:45
  75.3 4.2 %copy.77 = f32[96,8,1,96]{1,3,0,2:T(8,128)} copy(f32[96,8,1,96]{3,2,1,0:T(1,128)} %get-tuple-element.9) | data formatting | bytes 589824
  79.5 4.2 %copy.78 = f32[96,8,1,96]{1,3,0,2:T(8,128)} copy(f32[96,8,1,96]{3,2,1,0:T(1,128)} %get-tuple-element.7) | data formatting | bytes 589824
  83.7 6.9 %add.60 = f32[96,8,1,96]{1,3,0,2:T(8,128)} add(f32[96,8,1,96]{1,3,0,2:T(8,128)} %copy.77, f32[96,8,1,96]{1,3,0,2:T(8,128)} %copy.78) | non-fusion elementwise | flops 73728 | bytes 884736 | tf_op jit(solution)/shard_map/add | solution.py:43
  90.6 6.2 %copy.59 = f32[48,2,8,1,48,2]{4,2,5,3,1,0:T(8,128)} copy(f32[48,2,8,1,48,2]{2,5,4,1,0,3:T(2,128)} %bitcast.85) | data formatting | bytes 589824 | tf_op jit(solution)/shard_map/stack | solution.py:45
  99.3 9.3 %copy.74 = bf16[8,2,2,2,48,48]{0,3,2,1,5,4:T(2,128)(2,1)} copy(bf16[8,2,2,2,48,48]{5,0,3,1,2,4:T(8,128)(2,1)} %fusion.24) | data formatting | bytes 589824 | tf_op jit(solution)/shard_map/reshape | solution.py:51
  108.6 7.0 %reshape.131 = bf16[16,2,4608]{2,1,0:T(2,128)(2,1)} reshape(bf16[2304,2,2,2,8]{4,3,2,1,0:T(2,128)(2,1)} %bitcast.87) | data formatting | bytes 589824
  115.6 14.7 %all_to_all.60 = bf16[16,2,4608]{2,1,0:T(2,128)(2,1)} all-to-all(bf16[16,2,4608]{2,1,0:T(2,128)(2,1)} %reshape.131), channel_id=1, replica_groups=mesh['batch'=2,'rows'=16] {'rows'}, dimensions={0} | all-to-all | bytes 589824 | tf_op jit(solution)/shard_map/all_to_all | solution.py:124
  130.3 7.4 %reshape.132 = bf16[2304,2,2,2,8]{4,3,2,1,0:T(2,128)(2,1)} reshape(bf16[16,2,4608]{2,1,0:T(2,128)(2,1)} %all_to_all.60) | data formatting | bytes 589824
  137.7 12.1 %copy.75 = bf16[8,2,2,2,16,144]{5,4,0,3,2,1:T(8,128)(2,1)} copy(bf16[8,2,2,2,16,144]{0,3,2,1,5,4:T(2,128)(2,1)} %bitcast.88) | data formatting | bytes 589824 | tf_op jit(solution)/shard_map/all_to_all | solution.py:124
  167.1 4.2 %all-to-all-start.2 = ((bf16[64,2,2,2,144]{4,3,2,1,0:T(2,128)(2,1)}), bf16[64,2,2,2,144]{4,3,2,1,0:T(2,128)(2,1)}, u32[]{:S(2)}, u32[]{:S(2)}) async-start(bf16[64,2,2,2,144]{4,3,2,1,0:T(2,128)(2,1)} %bitcast.98), calls=%async_computation.2 | async-start | bytes 524288 | tf_op jit(solution)/shard_map/all_to_all | solution.py:133
  173.0 42.4 %psum.15 = f32[64,64]{1,0:T(8,128)} all-reduce(f32[64,64]{1,0:T(8,128)S(1)} %convolution_bitcast_fusion.1), channel_id=1, replica_groups=mesh['batch'=2,'rows'=16] {'batch','rows'}, use_global_device_ids=true, to_apply=%region_1.2 | all-reduce | flops 4096 | bytes 32768 | tf_op jit(solution)/shard_map/psum | solution.py:150
  219.3 13.9 %copy.69 = bf16[48,2,4,2,48,2]{2,5,4,3,1,0:T(2,128)(2,1)} copy(bf16[48,2,4,2,48,2]{4,0,5,1,3,2:T(8,128)(2,1)} %bitcast.89) | data formatting | bytes 294912 | tf_op jit(solution)/shard_map/transpose | solution.py:57
  233.2 8.4 %copy.68 = bf16[48,2,4,2,48,2]{5,4,3,2,1,0:T(8,128)(2,1)} copy(bf16[48,2,4,2,48,2]{4,0,5,1,3,2:T(8,128)(2,1)} %bitcast.90) | data formatting | bytes 294912 | tf_op jit(solution)/shard_map/transpose | solution.py:57
  247.6 4.9 %copy.70 = bf16[96,4,2,96]{3,2,1,0:T(2,128)(2,1)} copy(bf16[96,4,2,96]{1,3,2,0:T(8,128)(2,1)} %pad_maximum_fusion) | data formatting | bytes 294912 | tf_op jit(solution)/shard_map/stack | solution.py:83
  253.7 17.1 %concatenate.27 = bf16[96,768]{1,0:T(8,128)(2,1)} reshape(bf16[48,2,4,2,48,2]{5,4,3,2,1,0:T(8,128)(2,1)} %copy.68) | data formatting | bytes 294912 | tf_op jit(solution)/shard_map/concatenate | solution.py:84
  274.2 5.3 %all-to-all-start.3 = ((bf16[64,4,192]{2,1,0:T(4,128)(2,1)}), bf16[64,4,192]{2,1,0:T(4,128)(2,1)S(1)}, u32[]{:S(2)}, u32[]{:S(2)}) async-start(bf16[64,4,192]{2,1,0:T(4,128)(2,1)} %reshape.125), calls=%async_computation.3 | async-start | bytes 262144 | tf_op jit(solution)/shard_map/all_to_all | solution.py:138
  281.0 6.5 %all-to-all-done.3 = bf16[64,4,192]{2,1,0:T(4,128)(2,1)S(1)} async-done(((bf16[64,4,192]{2,1,0:T(4,128)(2,1)}), bf16[64,4,192]{2,1,0:T(4,128)(2,1)S(1)}, u32[]{:S(2)}, u32[]{:S(2)}) %all-to-all-start.3) | async-done | bytes 98336 | tf_op jit(solution)/shard_map/all_to_all | solution.py:138
  292.2 5.2 %copy.90 = f32[144,64,128]{2,1,0:T(8,128)} copy(f32[144,64,128]{2,1,0:T(8,128)} %all-reduce.2.cloned.1.call-done) | data formatting | bytes 9437184
  (75 shorter events, 71.8 us)
Async XLA Ops:
  7.2 154.9 %copy-start = (bf16[144,64,128]{2,1,0:T(8,128)(2,1)S(1)}, bf16[144,64,128]{2,1,0:T(8,128)(2,1)}, u32[]{:S(2)}) copy-start(bf16[144,64,128]{2,1,0:T(8,128)(2,1)} %param.11) | copy-start | bytes 7077892
  11.9 1.6 copy-start.4
  11.9 1.9 copy-start.5
  12.0 2.9 copy-start.6
  13.5 1.4 copy-start.1
  13.5 1.4 copy-start.2
  13.5 1.6 copy-start.3
  15.1 11.1 %copy-start.11 = (s32[1,32]{1,0:T(1,128)S(1)}, s32[1,32]{1,0:T(1,128)}, u32[]{:S(2)}) copy-start(s32[1,32]{1,0:T(1,128)} %param.12) | copy-start | bytes 388
  18.4 17.5 %all-to-all-start = ((bf16[4,128,192]{2,0,1:T(4,128)(2,1)}), bf16[4,128,192]{2,0,1:T(4,128)(2,1)}, u32[]{:S(2)}, u32[]{:S(2)}) async-start(bf16[4,128,192]{2,0,1:T(4,128)(2,1)} %copy.52), calls=%async_computation | async-start | bytes 524288 | tf_op jit(solution)/shard_map/all_to_all | solution.py:116
  25.9 266.3 %all-reduce.2.cloned.1.call-start = ((), (), s32[]{:S(2)}) async-start(), calls=%async_computation.4 | async-start | bytes 9437184 | tf_op jit(solution)/shard_map/psum | solution.py:132
  26.6 15.2 %copy-start.8 = (bf16[96,64]{1,0:T(8,128)(2,1)}, bf16[96,64]{1,0:T(8,128)(2,1)S(1)}, u32[]{:S(2)}) copy-start(bf16[96,64]{1,0:T(8,128)(2,1)S(1)} %get-tuple-element.15) | copy-start | bytes 36868
  26.6 15.2 %copy-start.9 = (bf16[96,64]{1,0:T(8,128)(2,1)}, bf16[96,64]{1,0:T(8,128)(2,1)S(1)}, u32[]{:S(2)}) copy-start(bf16[96,64]{1,0:T(8,128)(2,1)S(1)} %get-tuple-element.16) | copy-start | bytes 36868
  167.1 48.3 %all-to-all-start.2 = ((bf16[64,2,2,2,144]{4,3,2,1,0:T(2,128)(2,1)}), bf16[64,2,2,2,144]{4,3,2,1,0:T(2,128)(2,1)}, u32[]{:S(2)}, u32[]{:S(2)}) async-start(bf16[64,2,2,2,144]{4,3,2,1,0:T(2,128)(2,1)} %bitcast.98), calls=%async_computation.2 | async-start | bytes 524288 | tf_op jit(solution)/shard_map/all_to_all | solution.py:133
  272.5 18.2 %copy-start.10 = (bf16[64,64]{1,0:T(8,128)(2,1)S(1)}, bf16[64,64]{1,0:T(8,128)(2,1)}, u32[]{:S(2)}) copy-start(bf16[64,64]{1,0:T(8,128)(2,1)} %param.10) | copy-start | bytes 24580
  274.2 13.2 %all-to-all-start.3 = ((bf16[64,4,192]{2,1,0:T(4,128)(2,1)}), bf16[64,4,192]{2,1,0:T(4,128)(2,1)S(1)}, u32[]{:S(2)}, u32[]{:S(2)}) async-start(bf16[64,4,192]{2,1,0:T(4,128)(2,1)} %reshape.125), calls=%async_computation.3 | async-start | bytes 262144 | tf_op jit(solution)/shard_map/all_to_all | solution.py:138
  289.2 1.6 copy-start.7
Sparse Core Ops, SparseCore 0:
  162.2 119.0 all-reduce.1
where the time goes:
time: 309 us; the launch traced here: 304 us
  local copies, waits for them, and re-layouts  152 us (49%)
  blocking collectives  57.2 us (19%)
  other arithmetic  31.5 us (10%)
  starting transfers between devices  17.2 us (6%)
  matrix products  16.2 us (5%)
  waiting for transfers between devices  15.9 us (5%)
  between operations  14.3 us (5%)
    psum x1, blocking collectives, shards(): grad_weight = lax.psum(local_weight, ('batch', 'rows'))  42.4 us
    unnamed x31, local copies, waits for them, and re-layouts  36.7 us
    transpose x2, local copies, waits for them, and re-layouts, from_blocks(): shaped.transpose(4, 2, 0, 1, 5, 3)  22.3 us
    concatenate x2, local copies, waits for them, and re-layouts, row_adjoint(): joined = jnp.concatenate([upper, lower], axis=0)  18.2 us
    all_to_all x1, blocking collectives, shards(): lax.all_to_all(to_blocks(spectra, PA), 'rows', split_axis=4, concat_axis=...  14.7 us
    another operation x2, local copies, waits for them, and re-layouts, row_combine(): jnp.stack([real_part, imag_part], axis=2) * scale  12.3 us
    all_to_all x1, local copies, waits for them, and re-layouts, shards(): lax.all_to_all(to_blocks(spectra, PA), 'rows', split_axis=4, concat_axis=...  12.1 us
    all_to_all x1, waiting for transfers between devices, shards(): lax.all_to_all(colspec, 'rows', split_axis=1, concat_axis=0, tiled=True)  9.32 us
  transfers between devices with their start and end apart: 4, of which 2 were waited for; matrix products, arithmetic and copies ran while one was open for 24% of the time, Pallas kernels for 0%

commit v1 on v0

--- a/solution.py
+++ b/solution.py
@@ -147,7 +147,7 @@
         "ric,roc->rio", masked_in, grad_pre, preferred_element_type=jnp.float32
     )
     local_weight = jnp.sum(row_partial, axis=0)
-    grad_weight = lax.psum(local_weight, ("batch", "rows"))
+    grad_weight = lax.psum(lax.psum(local_weight, "rows"), "batch")
     grad_weight = grad_weight * (1.0 / math.sqrt(batch_devices * active * SLAB * column_count))
     return (grad_input, grad_spectral, grad_weight)
 

time: 309 us -> 336 us (1.087)
  blocking collectives: 57.2 us -> 86.3 us
    psum x1 -> x2, blocking collectives: 42.4 us -> 71.6 us  [shards(): grad_weight = lax.psum(lax.psum(local_weight, 'rows'), 'batch')]
  transfers between devices with their start and end apart: 4 -> 4, of which waited for: 2 -> 2; matrix products, arithmetic and copies ran while one was open for 24% -> 22% of each run, Pallas kernels for 0% -> 0%
where the time goes in v1:
time: 336 us; the launch traced here: 331 us
  local copies, waits for them, and re-layouts  152 us (45%)
  blocking collectives  86.3 us (26%)
  other arithmetic  31.5 us (9%)
  matrix products  16.2 us (5%)
  waiting for transfers between devices  15.8 us (5%)
  starting transfers between devices  15.4 us (5%)
  between operations  14.3 us (4%)
    psum x2, blocking collectives, shards(): grad_weight = lax.psum(lax.psum(local_weight, 'rows'), 'batch')  71.6 us
    unnamed x31, local copies, waits for them, and re-layouts  36.7 us
    transpose x2, local copies, waits for them, and re-layouts, from_blocks(): shaped.transpose(4, 2, 0, 1, 5, 3)  22.3 us
    concatenate x2, local copies, waits for them, and re-layouts, row_adjoint(): joined = jnp.concatenate([upper, lower], axis=0)  18.2 us
    all_to_all x1, blocking collectives, shards(): lax.all_to_all(to_blocks(spectra, PA), 'rows', split_axis=4, concat_axis=...  14.7 us
    another operation x2, local copies, waits for them, and re-layouts, row_combine(): jnp.stack([real_part, imag_part], axis=2) * scale  12.3 us
    all_to_all x1, local copies, waits for them, and re-layouts, shards(): lax.all_to_all(to_blocks(spectra, PA), 'rows', split_axis=4, concat_axis=...  12.1 us
    all_to_all x1, waiting for transfers between devices, shards(): lax.all_to_all(colspec, 'rows', split_axis=1, concat_axis=0, tiled=True)  9.32 us
  transfers between devices with their start and end apart: 4, of which 2 were waited for; matrix products, arithmetic and copies ran while one was open for 22% of the time, Pallas kernels for 0%

profile of v1, /device:TPU:0, one launch (start us, length us, event | category | flops | bytes accessed | tf_op | source)
XLA Modules:
  0.0 331.4 jit_solution(9082142591100739380)
XLA Ops:
  18.4 7.5 %all-to-all-start = ((bf16[4,128,192]{2,0,1:T(4,128)(2,1)}), bf16[4,128,192]{2,0,1:T(4,128)(2,1)}, u32[]{:S(2)}, u32[]{:S(2)}) async-start(bf16[4,128,192]{2,0,1:T(4,128)(2,1)} %copy.52), calls=%async_computation | async-start | bytes 524288 | tf_op jit(solution)/shard_map/all_to_all | solution.py:116
  26.6 9.3 %all-to-all-done = bf16[4,128,192]{2,0,1:T(4,128)(2,1)} async-done(((bf16[4,128,192]{2,0,1:T(4,128)(2,1)}), bf16[4,128,192]{2,0,1:T(4,128)(2,1)}, u32[]{:S(2)}, u32[]{:S(2)}) %all-to-all-start) | async-done | bytes 196640 | tf_op jit(solution)/shard_map/all_to_all | solution.py:116
  47.9 4.2 %copy.79 = f32[96,8,1,96]{1,3,0,2:T(8,128)} copy(f32[96,8,1,96]{3,2,1,0:T(1,128)} %get-tuple-element.10) | data formatting | bytes 589824
  58.0 4.2 %copy.80 = f32[96,8,1,96]{1,3,0,2:T(8,128)} copy(f32[96,8,1,96]{3,2,1,0:T(1,128)} %get-tuple-element.8) | data formatting | bytes 589824
  62.1 6.9 %sub.9 = f32[96,8,1,96]{1,3,0,2:T(8,128)} subtract(f32[96,8,1,96]{1,3,0,2:T(8,128)} %copy.79, f32[96,8,1,96]{1,3,0,2:T(8,128)} %copy.80) | non-fusion elementwise | flops 73728 | bytes 884736 | tf_op jit(solution)/shard_map/sub | solution.py:44
  69.1 6.2 %copy.60 = f32[48,2,8,1,48,2]{4,2,5,3,1,0:T(8,128)} copy(f32[48,2,8,1,48,2]{2,5,4,1,0,3:T(2,128)} %bitcast.84) | data formatting | bytes 589824 | tf_op jit(solution)/shard_map/stack | solution.py:45
  75.3 4.2 %copy.77 = f32[96,8,1,96]{1,3,0,2:T(8,128)} copy(f32[96,8,1,96]{3,2,1,0:T(1,128)} %get-tuple-element.9) | data formatting | bytes 589824
  79.4 4.2 %copy.78 = f32[96,8,1,96]{1,3,0,2:T(8,128)} copy(f32[96,8,1,96]{3,2,1,0:T(1,128)} %get-tuple-element.7) | data formatting | bytes 589824
  83.6 6.9 %add.62 = f32[96,8,1,96]{1,3,0,2:T(8,128)} add(f32[96,8,1,96]{1,3,0,2:T(8,128)} %copy.77, f32[96,8,1,96]{1,3,0,2:T(8,128)} %copy.78) | non-fusion elementwise | flops 73728 | bytes 884736 | tf_op jit(solution)/shard_map/add | solution.py:43
  90.5 6.2 %copy.59 = f32[48,2,8,1,48,2]{4,2,5,3,1,0:T(8,128)} copy(f32[48,2,8,1,48,2]{2,5,4,1,0,3:T(2,128)} %bitcast.85) | data formatting | bytes 589824 | tf_op jit(solution)/shard_map/stack | solution.py:45
  99.2 9.3 %copy.74 = bf16[8,2,2,2,48,48]{0,3,2,1,5,4:T(2,128)(2,1)} copy(bf16[8,2,2,2,48,48]{5,0,3,1,2,4:T(8,128)(2,1)} %fusion.24) | data formatting | bytes 589824 | tf_op jit(solution)/shard_map/reshape | solution.py:51
  108.6 6.9 %reshape.131 = bf16[16,2,4608]{2,1,0:T(2,128)(2,1)} reshape(bf16[2304,2,2,2,8]{4,3,2,1,0:T(2,128)(2,1)} %bitcast.87) | data formatting | bytes 589824
  115.5 14.7 %all_to_all.60 = bf16[16,2,4608]{2,1,0:T(2,128)(2,1)} all-to-all(bf16[16,2,4608]{2,1,0:T(2,128)(2,1)} %reshape.131), channel_id=1, replica_groups=mesh['batch'=2,'rows'=16] {'rows'}, dimensions={0} | all-to-all | bytes 589824 | tf_op jit(solution)/shard_map/all_to_all | solution.py:124
  130.2 7.4 %reshape.132 = bf16[2304,2,2,2,8]{4,3,2,1,0:T(2,128)(2,1)} reshape(bf16[16,2,4608]{2,1,0:T(2,128)(2,1)} %all_to_all.60) | data formatting | bytes 589824
  137.6 12.1 %copy.75 = bf16[8,2,2,2,16,144]{5,4,0,3,2,1:T(8,128)(2,1)} copy(bf16[8,2,2,2,16,144]{0,3,2,1,5,4:T(2,128)(2,1)} %bitcast.88) | data formatting | bytes 589824 | tf_op jit(solution)/shard_map/all_to_all | solution.py:124
  167.0 4.2 %all-to-all-start.2 = ((bf16[64,2,2,2,144]{4,3,2,1,0:T(2,128)(2,1)}), bf16[64,2,2,2,144]{4,3,2,1,0:T(2,128)(2,1)}, u32[]{:S(2)}, u32[]{:S(2)}) async-start(bf16[64,2,2,2,144]{4,3,2,1,0:T(2,128)(2,1)} %bitcast.98), calls=%async_computation.2 | async-start | bytes 524288 | tf_op jit(solution)/shard_map/all_to_all | solution.py:133
  172.9 61.8 %psum.22 = f32[64,64]{1,0:T(8,128)S(1)} all-reduce(f32[64,64]{1,0:T(8,128)S(1)} %convolution_bitcast_fusion.1), channel_id=1, replica_groups=mesh['batch'=2,'rows'=16] {'rows'}, use_global_device_ids=true, to_apply=%region_1.2 | all-reduce | flops 4096 | bytes 32768 | tf_op jit(solution)/shard_map/psum | solution.py:150
  234.6 9.8 %psum.23 = f32[64,64]{1,0:T(8,128)} all-reduce(f32[64,64]{1,0:T(8,128)S(1)} %psum.22), channel_id=1, replica_groups=mesh['batch'=2,'rows'=16] {'batch'}, use_global_device_ids=true, to_apply=%region_2.3 | all-reduce | flops 4096 | bytes 32768 | tf_op jit(solution)/shard_map/psum | solution.py:150
  248.4 13.8 %copy.69 = bf16[48,2,4,2,48,2]{2,5,4,3,1,0:T(2,128)(2,1)} copy(bf16[48,2,4,2,48,2]{4,0,5,1,3,2:T(8,128)(2,1)} %bitcast.89) | data formatting | bytes 294912 | tf_op jit(solution)/shard_map/transpose | solution.py:57
  262.3 8.4 %copy.68 = bf16[48,2,4,2,48,2]{5,4,3,2,1,0:T(8,128)(2,1)} copy(bf16[48,2,4,2,48,2]{4,0,5,1,3,2:T(8,128)(2,1)} %bitcast.90) | data formatting | bytes 294912 | tf_op jit(solution)/shard_map/transpose | solution.py:57
  276.7 4.8 %copy.70 = bf16[96,4,2,96]{3,2,1,0:T(2,128)(2,1)} copy(bf16[96,4,2,96]{1,3,2,0:T(8,128)(2,1)} %pad_maximum_fusion) | data formatting | bytes 294912 | tf_op jit(solution)/shard_map/stack | solution.py:83
  282.6 17.1 %concatenate.27 = bf16[96,768]{1,0:T(8,128)(2,1)} reshape(bf16[48,2,4,2,48,2]{5,4,3,2,1,0:T(8,128)(2,1)} %copy.68) | data formatting | bytes 294912 | tf_op jit(solution)/shard_map/concatenate | solution.py:84
  308.1 6.5 %all-to-all-done.3 = bf16[64,4,192]{2,1,0:T(4,128)(2,1)S(1)} async-done(((bf16[64,4,192]{2,1,0:T(4,128)(2,1)}), bf16[64,4,192]{2,1,0:T(4,128)(2,1)S(1)}, u32[]{:S(2)}, u32[]{:S(2)}) %all-to-all-start.3) | async-done | bytes 98336 | tf_op jit(solution)/shard_map/all_to_all | solution.py:138
  319.3 5.2 %copy.90 = f32[144,64,128]{2,1,0:T(8,128)} copy(f32[144,64,128]{2,1,0:T(8,128)} %all-reduce.2.cloned.1.call-done) | data formatting | bytes 9437184
  (76 shorter events, 75.2 us)
Async XLA Ops:
  7.2 154.8 %copy-start = (bf16[144,64,128]{2,1,0:T(8,128)(2,1)S(1)}, bf16[144,64,128]{2,1,0:T(8,128)(2,1)}, u32[]{:S(2)}) copy-start(bf16[144,64,128]{2,1,0:T(8,128)(2,1)} %param.11) | copy-start | bytes 7077892
  11.9 1.6 copy-start.4
  11.9 1.9 copy-start.5
  12.0 2.9 copy-start.6
  13.5 1.4 copy-start.1
  13.5 1.4 copy-start.2
  13.5 1.6 copy-start.3
  15.0 11.0 %copy-start.11 = (s32[1,32]{1,0:T(1,128)S(1)}, s32[1,32]{1,0:T(1,128)}, u32[]{:S(2)}) copy-start(s32[1,32]{1,0:T(1,128)} %param.12) | copy-start | bytes 388
  18.4 17.5 %all-to-all-start = ((bf16[4,128,192]{2,0,1:T(4,128)(2,1)}), bf16[4,128,192]{2,0,1:T(4,128)(2,1)}, u32[]{:S(2)}, u32[]{:S(2)}) async-start(bf16[4,128,192]{2,0,1:T(4,128)(2,1)} %copy.52), calls=%async_computation | async-start | bytes 524288 | tf_op jit(solution)/shard_map/all_to_all | solution.py:116
  25.9 293.4 %all-reduce.2.cloned.1.call-start = ((), (), s32[]{:S(2)}) async-start(), calls=%async_computation.4 | async-start | bytes 9437184 | tf_op jit(solution)/shard_map/psum | solution.py:132
  26.6 15.2 %copy-start.8 = (bf16[96,64]{1,0:T(8,128)(2,1)}, bf16[96,64]{1,0:T(8,128)(2,1)S(1)}, u32[]{:S(2)}) copy-start(bf16[96,64]{1,0:T(8,128)(2,1)S(1)} %get-tuple-element.15) | copy-start | bytes 36868
  26.6 15.2 %copy-start.9 = (bf16[96,64]{1,0:T(8,128)(2,1)}, bf16[96,64]{1,0:T(8,128)(2,1)S(1)}, u32[]{:S(2)}) copy-start(bf16[96,64]{1,0:T(8,128)(2,1)S(1)} %get-tuple-element.16) | copy-start | bytes 36868
  167.0 77.5 %all-to-all-start.2 = ((bf16[64,2,2,2,144]{4,3,2,1,0:T(2,128)(2,1)}), bf16[64,2,2,2,144]{4,3,2,1,0:T(2,128)(2,1)}, u32[]{:S(2)}, u32[]{:S(2)}) async-start(bf16[64,2,2,2,144]{4,3,2,1,0:T(2,128)(2,1)} %bitcast.98), calls=%async_computation.2 | async-start | bytes 524288 | tf_op jit(solution)/shard_map/all_to_all | solution.py:133
  301.5 16.4 %copy-start.10 = (bf16[64,64]{1,0:T(8,128)(2,1)S(1)}, bf16[64,64]{1,0:T(8,128)(2,1)}, u32[]{:S(2)}) copy-start(bf16[64,64]{1,0:T(8,128)(2,1)} %param.10) | copy-start | bytes 24580
  303.2 11.4 %all-to-all-start.3 = ((bf16[64,4,192]{2,1,0:T(4,128)(2,1)}), bf16[64,4,192]{2,1,0:T(4,128)(2,1)S(1)}, u32[]{:S(2)}, u32[]{:S(2)}) async-start(bf16[64,4,192]{2,1,0:T(4,128)(2,1)} %reshape.125), calls=%async_computation.3 | async-start | bytes 262144 | tf_op jit(solution)/shard_map/all_to_all | solution.py:138
  316.3 1.6 copy-start.7
Sparse Core Ops, SparseCore 0:
  162.1 118.3 all-reduce.1
